TPU v7x, 128 devices: a whole 4x4x4 slice. The times are simulated.
128 devices in a mesh: row: 8 (over x, core), col: 16 (over y, z).
Axes of the slice: x: 4, y: 4, z: 4, core: 2. Of those that a mesh axis runs over, the one named last changes fastest.
Arguments:
- series: bfloat16 [512, 32768], P(None, ('row', 'col')), may hold values from -6 to 6
- lag_weight: float32 [4], replicated, may hold values from 0.25 to 1
- start_basis: bfloat16 [64, 32768], P(None, ('row', 'col')), may hold values from -5.25 to 5.25
- block_pairs: int32 [8, 16, 32, 2], P('row', 'col'), may hold values from 0 to 127, as said below
- pair_count: int32 [8, 16], P('row', 'col'), may hold values from 1 to 32, as said below
Outputs:
- basis: float32 [64, 32768], P(None, ('row', 'col'))
- rayleigh: float32 [64, 64], replicated
Inputs may be any that keep to these rules, and one draw needn't show every extreme that they name: For every slot s of device (r, c), block_pairs[r, c, s, 0] is a block of row group r, from r * 16 to (r + 1) * 16 - 1, and block_pairs[r, c, s, 1] is a block held by a device of mesh column c: (block_pairs[r, c, s, 1]) mod (16) equals c. Slots that are not live hold blocks of the same ranges and are no part of the network. `pair_count`: the number of live slots of device (r, c); some device has exactly 32.
All inputs are finite; a program needn't handle non-finite values.
Results may differ from a plain program's by a relative error of at most 0.0045.
Values may be sent and summed in bfloat16 or wider, within the bound.
No kernel may reach another device: no remote copies, remote signals or barrier semaphores. Data moves between devices by JAX's collectives and lax.ppermute only.
A program may use at most 64 MiB of HBM per device.

v0:
```python
import math
import jax
import jax.numpy as jnp
from jax import lax
from jax.sharding import PartitionSpec as P

BLOCK = 256
ITERS = 2
BETA_CORR = 8.0
GRAM_EPS = 1e-05
HIGHEST = lax.Precision.HIGHEST


def lagged_tile(lead_block, trail_block, lag_weight, tile_scale):
    day_count = lead_block.shape[0]
    block_width = lead_block.shape[1]
    lag_count = lag_weight.shape[0]
    zero_rows = jnp.zeros((lag_count, block_width), lead_block.dtype)
    lead_padded = jnp.concatenate([lead_block, zero_rows], axis=0)
    trail_padded = jnp.concatenate([trail_block, zero_rows], axis=0)
    lead_shifted = jnp.concatenate(
        [lead_padded[offset : offset + day_count] for offset in range(lag_count)], axis=1
    )
    trail_shifted = jnp.concatenate(
        [trail_padded[offset : offset + day_count] for offset in range(lag_count)], axis=1
    )
    contract = (((0,), (0,)), ((), ()))
    forward = lax.dot_general(
        lead_shifted, trail_block, contract, preferred_element_type=jnp.float32
    )
    backward = lax.dot_general(
        lead_block, trail_shifted, contract, preferred_element_type=jnp.float32
    )
    forward = forward.reshape(lag_count, block_width, block_width)
    backward = jnp.transpose(backward.reshape(block_width, lag_count, block_width), (1, 0, 2))
    soft_corr = jnp.tanh(BETA_CORR / day_count * (forward + backward))
    weighted = jnp.sum(lag_weight[:, None, None] * soft_corr, axis=0)
    return (tile_scale * weighted).astype(jnp.bfloat16)


def local(series, lag_weight, start_basis, block_pairs, pair_count):
    n_rows = lax.axis_size("row")
    n_cols = lax.axis_size("col")
    row_index = lax.axis_index("row")
    local_cells = series.shape[1]
    local_blocks = local_cells // BLOCK
    row_blocks = local_blocks * n_cols
    col_blocks = local_blocks * n_rows
    slot_total = block_pairs.shape[2]
    cell_total = local_cells * n_rows * n_cols
    rank_size = start_basis.shape[0]
    tile_scale = 0.25 / math.sqrt(BLOCK)
    row_series = lax.all_gather(series, "col", axis=1, tiled=True)
    col_series = lax.all_gather(series, "row", axis=1, tiled=True)
    slot_pairs = block_pairs.reshape(slot_total, 2)
    slot_count = pair_count.reshape(1)
    row_first = row_index * row_blocks
    slot_ids = jnp.arange(slot_total, dtype=jnp.int32)
    own_rows = slot_pairs[:, 0] - row_first
    global_block = slot_pairs[:, 1]
    own_cols = global_block // local_blocks // n_cols * local_blocks + global_block % local_blocks
    built_count = slot_count[0]
    tile_rows = own_rows
    tile_cols = own_cols
    tile_rows = jnp.clip(tile_rows, 0, row_blocks - 1)
    tile_cols = jnp.clip(tile_cols, 0, col_blocks - 1)
    live_slots = slot_ids < built_count

    def build_one(slot, tiles):
        lead_block = lax.dynamic_slice_in_dim(row_series, tile_rows[slot] * BLOCK, BLOCK, 1)
        trail_block = lax.dynamic_slice_in_dim(col_series, tile_cols[slot] * BLOCK, BLOCK, 1)
        tile = lagged_tile(lead_block, trail_block, lag_weight, tile_scale)
        return lax.dynamic_update_index_in_dim(tiles, tile, slot, 0)

    tiles = lax.fori_loop(
        0, built_count, build_one, jnp.zeros((slot_total, BLOCK, BLOCK), jnp.bfloat16)
    )
    live_float = live_slots.astype(jnp.float32)[:, None]
    row_onehot = (tile_rows[:, None] == jnp.arange(row_blocks, dtype=jnp.int32)[None, :]).astype(
        jnp.float32
    ) * live_float
    col_onehot = (tile_cols[:, None] == jnp.arange(col_blocks, dtype=jnp.int32)[None, :]).astype(
        jnp.float32
    ) * live_float

    def project(basis_now):
        row_basis = lax.all_gather(basis_now, "col", axis=1, tiled=True).reshape(
            rank_size, row_blocks, BLOCK
        )
        col_basis = lax.all_gather(basis_now, "row", axis=1, tiled=True)
        col_basis = col_basis.reshape(rank_size, col_blocks, BLOCK)
        lead_basis = jnp.take(row_basis, tile_rows, axis=1)
        trail_basis = jnp.take(col_basis, tile_cols, axis=1)
        into_cols = jnp.einsum(
            "ksa,sab->ksb", lead_basis, tiles, preferred_element_type=jnp.float32
        )
        return (trail_basis, into_cols)

    def network_product(basis_now):
        trail_basis, into_cols = project(basis_now)
        into_rows = jnp.einsum(
            "ksb,sab->ksa", trail_basis, tiles, preferred_element_type=jnp.float32
        )
        row_part = jnp.einsum("ksa,sr->kra", into_rows, row_onehot, precision=HIGHEST)
        row_part = row_part.reshape(rank_size, row_blocks * BLOCK)
        col_part = jnp.einsum("ksb,sr->krb", into_cols, col_onehot, precision=HIGHEST)
        col_part = col_part.reshape(rank_size, col_blocks * BLOCK)
        row_total = lax.psum_scatter(row_part, "col", scatter_dimension=1, tiled=True)
        col_total = lax.psum_scatter(col_part, "row", scatter_dimension=1, tiled=True)
        return row_total + col_total

    current = start_basis
    basis = start_basis.astype(jnp.float32)
    for iteration in range(ITERS):
        product = network_product(current)
        local_gram = jnp.dot(product, product.T, precision=HIGHEST)
        gram = lax.psum(local_gram, ("row", "col")) / cell_total
        gram = gram + GRAM_EPS * jnp.eye(rank_size, dtype=jnp.float32)
        lower = jnp.linalg.cholesky(gram)
        basis = lax.linalg.triangular_solve(lower, product, left_side=True, lower=True)
        current = basis.astype(jnp.bfloat16)
    final = network_product(current)
    local_form = jnp.dot(final, current.astype(jnp.float32).T, precision=HIGHEST)
    rayleigh = lax.psum(local_form, ("row", "col")) / cell_total
    return (basis, rayleigh)


def solution(mesh):
    return jax.shard_map(
        local,
        mesh=mesh,
        in_specs=(
            P(None, ("row", "col")),
            P(),
            P(None, ("row", "col")),
            P("row", "col", None, None),
            P("row", "col"),
        ),
        out_specs=(P(None, ("row", "col")), P()),
        check_vma=False,
    )
```

profile of v0, /device:TPU:1, one launch (start us, length us, event | category | flops | bytes accessed | tf_op | source)
XLA Modules:
  0.0 914.3 jit_solution(11842656236986724844)
XLA Ops:
  8.0 0.7 all-gather.3.cloned.1.call-update
  8.7 14.7 %all_gather.26 = bf16[64,2048]{1,0:T(8,128)(2,1)S(1)} all-gather(bf16[64,256]{1,0:T(8,128)(2,1)} %param.16), channel_id=1, replica_groups=mesh['row'=8,'col'=16] {'row'}, dimensions={1}, use_global_device_ids=true | all-gather | bytes 294912 | tf_op jit(solution)/shard_map/all_gather | solution.py:90
  24.1 22.2 %all_gather.27 = bf16[64,4096]{1,0:T(8,128)(2,1)S(1)} all-gather(bf16[64,256]{1,0:T(8,128)(2,1)} %param.16), channel_id=1, replica_groups=mesh['row'=8,'col'=16] {'col'}, dimensions={1}, use_global_device_ids=true | all-gather | bytes 557056 | tf_op jit(solution)/shard_map/all_gather | solution.py:87
  47.1 51.3 %all-gather.3.cloned.1.call-done = bf16[512,4096]{1,0:T(8,128)(2,1)} async-done(((bf16[512,256]{1,0:T(8,128)(2,1)}), bf16[512,4096]{1,0:T(8,128)(2,1)}) %all-gather.3.cloned.1.call-update) | async-done | bytes 4194320 | tf_op jit(solution)/shard_map/all_gather | solution.py:53
  98.4 2.4 broadcast_in_dim.30
  100.8 116.0 %while.10 = (s32[]{:T(128)}, bf16[32,256,256]{2,1,0:T(8,128)(2,1)}, s32[]{:T(128)}, f32[4]{0:T(128)S(1)}, s32[32]{0:T(128)S(1)}, /*index=5*/bf16[512,4096]{1,0:T...) while((s32[]{:T(128)}, bf16[32,256,256]{2,1,0:T(8,128)(2,1)}, ...), condition=%wide.region_2.3_spmd, body=%wide.region_0.2_spmd.sunk | while | flops 546373632 | bytes 10617143 | solution.py:75
  104.0 1.1 constant_dynamic-slice_fusion.3
  110.4 1.1 constant_dynamic-slice_fusion.3
  116.8 1.1 constant_dynamic-slice_fusion.3
  123.2 1.1 constant_dynamic-slice_fusion.3
  129.6 1.1 constant_dynamic-slice_fusion.3
  136.0 1.1 constant_dynamic-slice_fusion.3
  142.4 1.1 constant_dynamic-slice_fusion.3
  148.8 1.1 constant_dynamic-slice_fusion.3
  155.2 1.1 constant_dynamic-slice_fusion.3
  161.6 1.1 constant_dynamic-slice_fusion.3
  168.0 1.1 constant_dynamic-slice_fusion.3
  174.4 1.1 constant_dynamic-slice_fusion.3
  180.9 1.1 constant_dynamic-slice_fusion.3
  187.3 1.1 constant_dynamic-slice_fusion.3
  193.7 1.1 constant_dynamic-slice_fusion.3
  200.1 1.1 constant_dynamic-slice_fusion.3
  206.5 1.1 constant_dynamic-slice_fusion.3
  212.9 1.1 constant_dynamic-slice_fusion.3
  216.8 3.1 convolution_bitcast_fusion.2
  219.9 2.2 fusion.33
  222.1 1.0 copy.55
  223.8 3.6 convolution_bitcast_fusion.5
  227.4 2.2 fusion.35
  229.6 1.6 copy.54
  231.3 105.0 %reduce-scatter.9.cloned.1.call-done = f32[64,256]{1,0:T(8,128)} async-done(((f32[64,2048]{1,0:T(8,128)}), f32[64,256]{1,0:T(8,128)}) %reduce-scatter.9.cloned.1.call-update) | async-done | bytes 65552 | tf_op jit(solution)/shard_map/reduce_scatter | solution.py:109
  336.4 76.9 %reduce-scatter.7.cloned.1.call-done = f32[64,256]{1,0:T(8,128)} async-done(((f32[64,4096]{1,0:T(8,128)}), f32[64,256]{1,0:T(8,128)}) %reduce-scatter.7.cloned.1.call-update) | async-done | bytes 65552 | tf_op jit(solution)/shard_map/reduce_scatter | solution.py:108
  413.3 0.9 add.86
  414.3 66.1 %psum.21 = f32[64,64]{0,1:T(8,128)S(1)} all-reduce(f32[64,64]{0,1:T(8,128)S(1)} %fusion.117), channel_id=1, replica_groups=mesh['row'=8,'col'=16] {'row','col'}, use_global_device_ids=true, to_apply=%region_5.8 | all-reduce | flops 4096 | bytes 32768 | tf_op jit(solution)/shard_map/psum | solution.py:117
  480.6 5.8 cholesky.44
  487.8 4.9 custom-call.6
  493.0 17.4 %all_gather.29 = bf16[64,4096]{1,0:T(8,128)(2,1)S(1)} all-gather(bf16[64,256]{1,0:T(8,128)(2,1)S(1)} %convolution_convert_fusion), channel_id=1, replica_groups=mesh['row'=8,'col'=16] {'col'}, dimensions={1}, use_global_device_ids=true | all-gather | bytes 557056 | tf_op jit(solution)/shard_map/all_gather | solution.py:87
  511.0 3.1 convolution_bitcast_fusion.1
  514.1 2.2 fusion.29
  516.3 1.0 copy.57
  517.4 18.7 %all_gather.28 = bf16[64,2048]{1,0:T(8,128)(2,1)S(1)} all-gather(bf16[64,256]{1,0:T(8,128)(2,1)S(1)} %convolution_convert_fusion), channel_id=1, replica_groups=mesh['row'=8,'col'=16] {'row'}, dimensions={1}, use_global_device_ids=true | all-gather | bytes 294912 | tf_op jit(solution)/shard_map/all_gather | solution.py:90
  536.7 3.6 convolution_bitcast_fusion.4
  540.3 2.2 fusion.31
  542.5 1.6 copy.56
  544.2 5.1 reduce-scatter.13.cloned.1.call-done
  549.3 76.8 %reduce-scatter.11.cloned.1.call-done = f32[64,256]{1,0:T(8,128)} async-done(((f32[64,4096]{1,0:T(8,128)}), f32[64,256]{1,0:T(8,128)}) %reduce-scatter.11.cloned.1.call-update) | async-done | bytes 65552 | tf_op jit(solution)/shard_map/reduce_scatter | solution.py:108
  626.1 0.9 add.88
  627.2 66.2 %psum.22 = f32[64,64]{0,1:T(8,128)S(1)} all-reduce(f32[64,64]{0,1:T(8,128)S(1)} %fusion.118), channel_id=1, replica_groups=mesh['row'=8,'col'=16] {'row','col'}, use_global_device_ids=true, to_apply=%region_10.15 | all-reduce | flops 4096 | bytes 32768 | tf_op jit(solution)/shard_map/psum | solution.py:117
  693.5 5.8 cholesky.55
  700.7 4.9 custom-call.7
  705.6 0.9 fusion.116
  706.5 17.4 %all_gather.31 = bf16[64,4096]{1,0:T(8,128)(2,1)S(1)} all-gather(bf16[64,256]{1,0:T(8,128)(2,1)S(1)} %get-tuple-element.86), channel_id=1, replica_groups=mesh['row'=8,'col'=16] {'col'}, dimensions={1}, use_global_device_ids=true | all-gather | bytes 557056 | tf_op jit(solution)/shard_map/all_gather | solution.py:87
  724.5 3.1 convolution_bitcast_fusion
  727.6 2.2 fusion.25
  729.8 1.0 copy.59
  730.9 18.6 %all_gather.30 = bf16[64,2048]{1,0:T(8,128)(2,1)S(1)} all-gather(bf16[64,256]{1,0:T(8,128)(2,1)S(1)} %get-tuple-element.86), channel_id=1, replica_groups=mesh['row'=8,'col'=16] {'row'}, dimensions={1}, use_global_device_ids=true | all-gather | bytes 294912 | tf_op jit(solution)/shard_map/all_gather | solution.py:90
  750.2 3.6 convolution_bitcast_fusion.3
  753.8 2.2 fusion.27
  756.0 1.6 copy.58
  757.6 5.1 reduce-scatter.17.cloned.1.call-done
  762.7 77.0 %reduce-scatter.15.cloned.1.call-done = f32[64,256]{1,0:T(8,128)} async-done(((f32[64,4096]{1,0:T(8,128)}), f32[64,256]{1,0:T(8,128)}) %reduce-scatter.15.cloned.1.call-update) | async-done | bytes 65552 | tf_op jit(solution)/shard_map/reduce_scatter | solution.py:108
  839.7 1.0 fusion.61
  840.8 66.0 %psum.23 = f32[64,64]{0,1:T(8,128)S(1)} all-reduce(f32[64,64]{0,1:T(8,128)S(1)} %fusion.61), channel_id=1, replica_groups=mesh['row'=8,'col'=16] {'row','col'}, use_global_device_ids=true, to_apply=%region_13.18 | all-reduce | flops 4096 | bytes 32768 | tf_op jit(solution)/shard_map/psum | solution.py:124
  906.8 0.7 copy.43
  (199 shorter events, 68.4 us)
Async XLA Ops:
  7.2 39.2 %copy-start.1 = (s32[1,1,32,2]{2,3,1,0:T(2,128)S(1)}, s32[1,1,32,2]{2,3,1,0:T(2,128)}, u32[]{:S(2)}) copy-start(s32[1,1,32,2]{2,3,1,0:T(2,128)} %param.17) | copy-start | bytes 772
  7.2 39.9 %all-gather.5.cloned.1.call-start = ((), (), s32[]{:S(2)}) async-start(), calls=%async_computation.7 | async-start | bytes 2359296 | tf_op jit(solution)/shard_map/all_gather | solution.py:54
  7.9 90.4 %all-gather.3.cloned.1.call-start = ((), (), s32[]{:S(2)}) async-start(), calls=%async_computation.6 | async-start | bytes 4456448 | tf_op jit(solution)/shard_map/all_gather | solution.py:53
  8.7 327.7 %reduce-scatter.9.cloned.1.call-start = ((), (), s32[]{:S(2)}) async-start(), calls=%async_computation.9 | async-start | bytes 589824 | tf_op jit(solution)/shard_map/reduce_scatter | solution.py:109
  98.4 2.4 copy-start
  223.1 190.1 %reduce-scatter.7.cloned.1.call-start = ((), (), s32[]{:S(2)}) async-start(), calls=%async_computation.8 | async-start | bytes 1114112 | tf_op jit(solution)/shard_map/reduce_scatter | solution.py:108
  231.3 318.0 %reduce-scatter.13.cloned.1.call-start = ((), (), s32[]{:S(2)}) async-start(), calls=%async_computation.11 | async-start | bytes 589824 | tf_op jit(solution)/shard_map/reduce_scatter | solution.py:109
  517.3 108.8 %reduce-scatter.11.cloned.1.call-start = ((), (), s32[]{:S(2)}) async-start(), calls=%async_computation.10 | async-start | bytes 1114112 | tf_op jit(solution)/shard_map/reduce_scatter | solution.py:108
  544.2 218.6 %reduce-scatter.17.cloned.1.call-start = ((), (), s32[]{:S(2)}) async-start(), calls=%async_computation.13 | async-start | bytes 589824 | tf_op jit(solution)/shard_map/reduce_scatter | solution.py:109
  730.8 108.9 %reduce-scatter.15.cloned.1.call-start = ((), (), s32[]{:S(2)}) async-start(), calls=%async_computation.12 | async-start | bytes 1114112 | tf_op jit(solution)/shard_map/reduce_scatter | solution.py:108
Sparse Core Ops, SparseCore 0:
  9.7 30.3 all-gather.4
  42.1 56.1 all-gather.2
  223.2 113.0 reduce-scatter.8
  339.4 73.7 reduce-scatter.6
  517.5 31.7 reduce-scatter.12
  552.3 73.7 reduce-scatter.10
  731.0 31.7 reduce-scatter.16
  765.9 73.7 reduce-scatter.14
where the time goes:
time: 917 us; the launch traced here: 914 us
  waiting for transfers between devices  399 us (44%)
  blocking collectives  307 us (33%)
  local copies, waits for them, and re-layouts  61.1 us (7%)
  matrix products  52.8 us (6%)
  other arithmetic  42.2 us (5%)
  loops' own time  36.9 us (4%)
  between operations  15.1 us (2%)
    reduce_scatter x3, waiting for transfers between devices, network_product(): lax.psum_scatter(row_part, 'col', scatter_dimension=1, tiled=True)  231 us
    psum x2, blocking collectives, local(): gram = lax.psum(local_gram, ('row', 'col')) / cell_total  132 us
    reduce_scatter x3, waiting for transfers between devices, network_product(): lax.psum_scatter(col_part, 'row', scatter_dimension=1, tiled=True)  115 us
    psum x1, blocking collectives, local(): rayleigh = lax.psum(local_form, ('row', 'col')) / cell_total  66 us
    all_gather x3, blocking collectives, project(): lax.all_gather(basis_now, 'col', axis=1, tiled=True)  56.9 us
    all_gather x3, blocking collectives, project(): col_basis = lax.all_gather(basis_now, 'row', axis=1, tiled=True)  52 us
    all_gather x1, waiting for transfers between devices, local(): row_series = lax.all_gather(series, 'col', axis=1, tiled=True)  51.3 us
    another operation x1, loops' own time, local(): lax.fori_loop(0, built_count, build_one, jnp.zeros((slot_total, BLOCK, BL...  36.9 us
  transfers between devices with their start and end apart: 8, of which 7 were waited for; matrix products, arithmetic and copies ran while one was open for 3% of the time, Pallas kernels for 0%

commit v1 on v0

--- a/solution.py
+++ b/solution.py
@@ -121,7 +121,7 @@
         current = basis.astype(jnp.bfloat16)
     final = network_product(current)
     local_form = jnp.dot(final, current.astype(jnp.float32).T, precision=HIGHEST)
-    rayleigh = lax.psum(local_form, ("row", "col")) / cell_total
+    rayleigh = lax.psum(lax.psum(local_form, "col"), "row") / cell_total
     return (basis, rayleigh)
 
 

time: 917 us -> 947 us (1.033)
  blocking collectives: 307 us -> 336 us
    psum x1 -> x2, blocking collectives: 66 us -> 94.5 us  [local(): rayleigh = lax.psum(lax.psum(local_form, 'col'), 'row') / cell_total]
where the time goes in v1:
time: 947 us; the launch traced here: 943 us
  waiting for transfers between devices  399 us (42%)
  blocking collectives  336 us (35%)
  local copies, waits for them, and re-layouts  61.1 us (6%)
  matrix products  52.8 us (6%)
  other arithmetic  42.2 us (4%)
  loops' own time  36.9 us (4%)
  between operations  15.1 us (2%)
    reduce_scatter x3, waiting for transfers between devices, network_product(): lax.psum_scatter(row_part, 'col', scatter_dimension=1, tiled=True)  231 us
    psum x2, blocking collectives, local(): gram = lax.psum(local_gram, ('row', 'col')) / cell_total  132 us
    reduce_scatter x3, waiting for transfers between devices, network_product(): lax.psum_scatter(col_part, 'row', scatter_dimension=1, tiled=True)  115 us
    psum x2, blocking collectives, local(): rayleigh = lax.psum(lax.psum(local_form, 'col'), 'row') / cell_total  94.5 us
    all_gather x3, blocking collectives, project(): lax.all_gather(basis_now, 'col', axis=1, tiled=True)  56.9 us
    all_gather x3, blocking collectives, project(): col_basis = lax.all_gather(basis_now, 'row', axis=1, tiled=True)  52 us
    all_gather x1, waiting for transfers between devices, local(): row_series = lax.all_gather(series, 'col', axis=1, tiled=True)  51.3 us
    another operation x1, loops' own time, local(): lax.fori_loop(0, built_count, build_one, jnp.zeros((slot_total, BLOCK, BL...  36.9 us
  transfers between devices with their start and end apart: 8, of which 7 were waited for; matrix products, arithmetic and copies ran while one was open for 3% of the time, Pallas kernels for 0%

profile of v1, /device:TPU:1, one launch (start us, length us, event | category | flops | bytes accessed | tf_op | source)
XLA Modules:
  0.0 942.8 jit_solution(4889714485644341192)
XLA Ops:
  8.7 14.7 %all_gather.26 = bf16[64,2048]{1,0:T(8,128)(2,1)S(1)} all-gather(bf16[64,256]{1,0:T(8,128)(2,1)} %param.16), channel_id=1, replica_groups=mesh['row'=8,'col'=16] {'row'}, dimensions={1}, use_global_device_ids=true | all-gather | bytes 294912 | tf_op jit(solution)/shard_map/all_gather | solution.py:90
  24.1 22.2 %all_gather.27 = bf16[64,4096]{1,0:T(8,128)(2,1)S(1)} all-gather(bf16[64,256]{1,0:T(8,128)(2,1)} %param.16), channel_id=1, replica_groups=mesh['row'=8,'col'=16] {'col'}, dimensions={1}, use_global_device_ids=true | all-gather | bytes 557056 | tf_op jit(solution)/shard_map/all_gather | solution.py:87
  47.1 51.3 %all-gather.3.cloned.1.call-done = bf16[512,4096]{1,0:T(8,128)(2,1)} async-done(((bf16[512,256]{1,0:T(8,128)(2,1)}), bf16[512,4096]{1,0:T(8,128)(2,1)}) %all-gather.3.cloned.1.call-update) | async-done | bytes 4194320 | tf_op jit(solution)/shard_map/all_gather | solution.py:53
  98.4 2.4 broadcast_in_dim.30
  100.8 116.0 %while.10 = (s32[]{:T(128)}, bf16[32,256,256]{2,1,0:T(8,128)(2,1)}, s32[]{:T(128)}, f32[4]{0:T(128)S(1)}, s32[32]{0:T(128)S(1)}, /*index=5*/bf16[512,4096]{1,0:T...) while((s32[]{:T(128)}, bf16[32,256,256]{2,1,0:T(8,128)(2,1)}, ...), condition=%wide.region_2.3_spmd, body=%wide.region_0.2_spmd.sunk | while | flops 546373632 | bytes 10617143 | solution.py:75
  104.0 1.1 constant_dynamic-slice_fusion.3
  110.4 1.1 constant_dynamic-slice_fusion.3
  116.8 1.1 constant_dynamic-slice_fusion.3
  123.2 1.1 constant_dynamic-slice_fusion.3
  129.6 1.1 constant_dynamic-slice_fusion.3
  136.0 1.1 constant_dynamic-slice_fusion.3
  142.4 1.1 constant_dynamic-slice_fusion.3
  148.8 1.1 constant_dynamic-slice_fusion.3
  155.2 1.1 constant_dynamic-slice_fusion.3
  161.6 1.1 constant_dynamic-slice_fusion.3
  168.0 1.1 constant_dynamic-slice_fusion.3
  174.4 1.1 constant_dynamic-slice_fusion.3
  180.9 1.1 constant_dynamic-slice_fusion.3
  187.3 1.1 constant_dynamic-slice_fusion.3
  193.7 1.1 constant_dynamic-slice_fusion.3
  200.1 1.1 constant_dynamic-slice_fusion.3
  206.5 1.1 constant_dynamic-slice_fusion.3
  212.9 1.1 constant_dynamic-slice_fusion.3
  216.8 3.1 convolution_bitcast_fusion.2
  219.9 2.2 fusion.33
  222.1 1.0 copy.55
  223.8 3.6 convolution_bitcast_fusion.5
  227.4 2.2 fusion.35
  229.6 1.6 copy.54
  231.3 105.0 %reduce-scatter.9.cloned.1.call-done = f32[64,256]{1,0:T(8,128)} async-done(((f32[64,2048]{1,0:T(8,128)}), f32[64,256]{1,0:T(8,128)}) %reduce-scatter.9.cloned.1.call-update) | async-done | bytes 65552 | tf_op jit(solution)/shard_map/reduce_scatter | solution.py:109
  336.4 76.9 %reduce-scatter.7.cloned.1.call-done = f32[64,256]{1,0:T(8,128)} async-done(((f32[64,4096]{1,0:T(8,128)}), f32[64,256]{1,0:T(8,128)}) %reduce-scatter.7.cloned.1.call-update) | async-done | bytes 65552 | tf_op jit(solution)/shard_map/reduce_scatter | solution.py:108
  413.3 0.9 add.88
  414.3 66.1 %psum.28 = f32[64,64]{0,1:T(8,128)S(1)} all-reduce(f32[64,64]{0,1:T(8,128)S(1)} %fusion.117), channel_id=1, replica_groups=mesh['row'=8,'col'=16] {'row','col'}, use_global_device_ids=true, to_apply=%region_5.8 | all-reduce | flops 4096 | bytes 32768 | tf_op jit(solution)/shard_map/psum | solution.py:117
  480.6 5.8 cholesky.44
  487.8 4.9 custom-call.6
  493.0 17.4 %all_gather.29 = bf16[64,4096]{1,0:T(8,128)(2,1)S(1)} all-gather(bf16[64,256]{1,0:T(8,128)(2,1)S(1)} %convolution_convert_fusion), channel_id=1, replica_groups=mesh['row'=8,'col'=16] {'col'}, dimensions={1}, use_global_device_ids=true | all-gather | bytes 557056 | tf_op jit(solution)/shard_map/all_gather | solution.py:87
  511.0 3.1 convolution_bitcast_fusion.1
  514.1 2.2 fusion.29
  516.3 1.0 copy.57
  517.4 18.7 %all_gather.28 = bf16[64,2048]{1,0:T(8,128)(2,1)S(1)} all-gather(bf16[64,256]{1,0:T(8,128)(2,1)S(1)} %convolution_convert_fusion), channel_id=1, replica_groups=mesh['row'=8,'col'=16] {'row'}, dimensions={1}, use_global_device_ids=true | all-gather | bytes 294912 | tf_op jit(solution)/shard_map/all_gather | solution.py:90
  536.7 3.6 convolution_bitcast_fusion.4
  540.3 2.2 fusion.31
  542.5 1.6 copy.56
  544.2 5.1 reduce-scatter.13.cloned.1.call-done
  549.3 76.8 %reduce-scatter.11.cloned.1.call-done = f32[64,256]{1,0:T(8,128)} async-done(((f32[64,4096]{1,0:T(8,128)}), f32[64,256]{1,0:T(8,128)}) %reduce-scatter.11.cloned.1.call-update) | async-done | bytes 65552 | tf_op jit(solution)/shard_map/reduce_scatter | solution.py:108
  626.1 0.9 add.90
  627.2 66.2 %psum.29 = f32[64,64]{0,1:T(8,128)S(1)} all-reduce(f32[64,64]{0,1:T(8,128)S(1)} %fusion.118), channel_id=1, replica_groups=mesh['row'=8,'col'=16] {'row','col'}, use_global_device_ids=true, to_apply=%region_10.15 | all-reduce | flops 4096 | bytes 32768 | tf_op jit(solution)/shard_map/psum | solution.py:117
  693.5 5.8 cholesky.55
  700.7 4.9 custom-call.7
  705.6 0.9 fusion.116
  706.5 17.4 %all_gather.31 = bf16[64,4096]{1,0:T(8,128)(2,1)S(1)} all-gather(bf16[64,256]{1,0:T(8,128)(2,1)S(1)} %get-tuple-element.86), channel_id=1, replica_groups=mesh['row'=8,'col'=16] {'col'}, dimensions={1}, use_global_device_ids=true | all-gather | bytes 557056 | tf_op jit(solution)/shard_map/all_gather | solution.py:87
  724.5 3.1 convolution_bitcast_fusion
  727.6 2.2 fusion.25
  729.8 1.0 copy.59
  730.9 18.6 %all_gather.30 = bf16[64,2048]{1,0:T(8,128)(2,1)S(1)} all-gather(bf16[64,256]{1,0:T(8,128)(2,1)S(1)} %get-tuple-element.86), channel_id=1, replica_groups=mesh['row'=8,'col'=16] {'row'}, dimensions={1}, use_global_device_ids=true | all-gather | bytes 294912 | tf_op jit(solution)/shard_map/all_gather | solution.py:90
  750.2 3.6 convolution_bitcast_fusion.3
  753.8 2.2 fusion.27
  756.0 1.6 copy.58
  757.6 5.1 reduce-scatter.17.cloned.1.call-done
  762.7 77.0 %reduce-scatter.15.cloned.1.call-done = f32[64,256]{1,0:T(8,128)} async-done(((f32[64,4096]{1,0:T(8,128)}), f32[64,256]{1,0:T(8,128)}) %reduce-scatter.15.cloned.1.call-update) | async-done | bytes 65552 | tf_op jit(solution)/shard_map/reduce_scatter | solution.py:108
  839.7 1.0 fusion.61
  840.8 57.9 %psum.30 = f32[64,64]{0,1:T(8,128)S(1)} all-reduce(f32[64,64]{0,1:T(8,128)S(1)} %fusion.61), channel_id=1, replica_groups=mesh['row'=8,'col'=16] {'col'}, use_global_device_ids=true, to_apply=%region_13.18 | all-reduce | flops 4096 | bytes 32768 | tf_op jit(solution)/shard_map/psum | solution.py:124
  898.7 36.6 %psum.31 = f32[64,64]{0,1:T(8,128)S(1)} all-reduce(f32[64,64]{0,1:T(8,128)S(1)} %psum.30), channel_id=1, replica_groups=mesh['row'=8,'col'=16] {'row'}, use_global_device_ids=true, to_apply=%region_14.19 | all-reduce | flops 4096 | bytes 32768 | tf_op jit(solution)/shard_map/psum | solution.py:124
  935.3 0.7 copy.43
  (200 shorter events, 69.1 us)
Async XLA Ops:
  7.2 39.2 %copy-start.1 = (s32[1,1,32,2]{2,3,1,0:T(2,128)S(1)}, s32[1,1,32,2]{2,3,1,0:T(2,128)}, u32[]{:S(2)}) copy-start(s32[1,1,32,2]{2,3,1,0:T(2,128)} %param.17) | copy-start | bytes 772
  7.2 39.9 %all-gather.5.cloned.1.call-start = ((), (), s32[]{:S(2)}) async-start(), calls=%async_computation.7 | async-start | bytes 2359296 | tf_op jit(solution)/shard_map/all_gather | solution.py:54
  7.9 90.4 %all-gather.3.cloned.1.call-start = ((), (), s32[]{:S(2)}) async-start(), calls=%async_computation.6 | async-start | bytes 4456448 | tf_op jit(solution)/shard_map/all_gather | solution.py:53
  8.7 327.7 %reduce-scatter.9.cloned.1.call-start = ((), (), s32[]{:S(2)}) async-start(), calls=%async_computation.9 | async-start | bytes 589824 | tf_op jit(solution)/shard_map/reduce_scatter | solution.py:109
  98.4 2.4 copy-start
  223.1 190.1 %reduce-scatter.7.cloned.1.call-start = ((), (), s32[]{:S(2)}) async-start(), calls=%async_computation.8 | async-start | bytes 1114112 | tf_op jit(solution)/shard_map/reduce_scatter | solution.py:108
  231.3 318.0 %reduce-scatter.13.cloned.1.call-start = ((), (), s32[]{:S(2)}) async-start(), calls=%async_computation.11 | async-start | bytes 589824 | tf_op jit(solution)/shard_map/reduce_scatter | solution.py:109
  517.3 108.8 %reduce-scatter.11.cloned.1.call-start = ((), (), s32[]{:S(2)}) async-start(), calls=%async_computation.10 | async-start | bytes 1114112 | tf_op jit(solution)/shard_map/reduce_scatter | solution.py:108
  544.2 218.6 %reduce-scatter.17.cloned.1.call-start = ((), (), s32[]{:S(2)}) async-start(), calls=%async_computation.13 | async-start | bytes 589824 | tf_op jit(solution)/shard_map/reduce_scatter | solution.py:109
  730.8 108.9 %reduce-scatter.15.cloned.1.call-start = ((), (), s32[]{:S(2)}) async-start(), calls=%async_computation.12 | async-start | bytes 1114112 | tf_op jit(solution)/shard_map/reduce_scatter | solution.py:108
Sparse Core Ops, SparseCore 0:
  9.7 30.3 all-gather.4
  42.1 56.1 all-gather.2
  223.2 113.0 reduce-scatter.8
  339.4 73.7 reduce-scatter.6
  517.5 31.7 reduce-scatter.12
  552.3 73.7 reduce-scatter.10
  731.0 31.7 reduce-scatter.16
  765.9 73.7 reduce-scatter.14
